TPU v7x, 32 devices: a whole 2x2x4 slice. The times are simulated.
32 devices in a mesh: prow: 4 (over z), pcol: 8 (over y, x, core).
Axes of the slice: x: 2, y: 2, z: 4, core: 2. Of those that a mesh axis runs over, the one named last changes fastest.
Arguments:
- matrix: float32 [6, 4, 256, 3, 8, 256], P(None, 'prow', None, None, 'pcol'), may hold values from -6 to 6
- row_order: int32 [6144], replicated, may hold values from 0 to 6143, as said below
- inverses: float32 [4, 256, 256], replicated, may hold values from -0.0234375 to 0.0234375
- lower_fill: int32 [4, 24], replicated, may hold values 0 or 1
- upper_fill: int32 [4, 24], replicated, may hold values 0 or 1
Outputs:
- factored: float32 [6, 4, 256, 3, 8, 256], P(None, 'prow', None, None, 'pcol')
Inputs may be any that keep to these rules, and one draw needn't show every extreme that they name: row_order is a permutation of the rows; of the rows whose block row index is congruent to p modulo the number of indices of prow, exactly 6 * 256 divided by that number go to rows whose block row index is congruent to s, for every p and s.
All inputs are finite; a program needn't handle non-finite values.
Results may differ from a plain program's by a relative error of at most 0.0002.
Values sent between devices are 32-bit elements; how exact they have to be, the bound alone decides.
A program may use at most 128 MiB of HBM per device.

v0:
```python
import functools

import jax
import jax.numpy as jnp
from jax import lax
from jax.experimental import pallas as pl
from jax.experimental.pallas import tpu as pltpu
from jax.sharding import PartitionSpec as P


def mm(a, b):
    return jnp.dot(a, b, precision=lax.Precision.HIGH, preferred_element_type=jnp.float32)


def index_lists(row_order, rows, width, prows, here_row):
    local_rows = rows * width
    blocks = row_order.reshape(rows, prows, width)
    targets = lax.dynamic_index_in_dim(blocks, here_row, 1, keepdims=False).reshape(-1)
    local = jnp.arange(local_rows, dtype=jnp.int32)
    sending = jnp.sort((targets // width % prows) * local_rows + local) % local_rows
    by_source = jnp.transpose(blocks, (1, 0, 2)).reshape(-1)
    dest_local = by_source // width // prows * width + by_source % width
    mine = by_source // width % prows == here_row
    position = jnp.cumsum(mine.astype(jnp.int32)) - 1
    key = jnp.where(mine, dest_local * local_rows + position, local_rows * local_rows)
    taking = jnp.sort(key)[:local_rows] % local_rows
    return sending, taking


def keep_of(fill_row, panel, blocks):
    return (blocks > panel) & (fill_row[blocks] == 1)


def body(matrix, row_order, inverses, lower_fill, upper_fill):
    nrows = matrix.shape[0]
    width = matrix.shape[2]
    ncols = matrix.shape[3]
    prows = lax.axis_size("prow")
    pcols = lax.axis_size("pcol")
    p = lax.axis_index("prow")
    q = lax.axis_index("pcol")
    panels = inverses.shape[0]
    local_rows = nrows * width
    cols = ncols * width
    sending, taking = index_lists(row_order, nrows, width, prows, p)
    work = matrix.reshape(local_rows, cols)
    outgoing = work[sending].reshape(prows, local_rows // prows, cols)
    incoming = lax.all_to_all(outgoing, "prow", split_axis=0, concat_axis=0, tiled=True)
    work = incoming.reshape(local_rows, cols)[taking]
    tops = lax.all_gather(work[:width], "prow", axis=0, tiled=False)[:panels]
    tops = tops.reshape(panels * width, cols)
    column = jnp.concatenate([tops[:, :width], work[:, :width]], axis=0)
    ratio = pcols // panels
    pieces = column.reshape(ratio, -1, width)
    piece = jnp.where(q < panels, pieces[0], 0.0)
    for j in range(1, ratio):
        pairs = [(k, k + panels * j) for k in range(panels)]
        piece = piece + lax.ppermute(pieces[j], "pcol", pairs)
    every = lax.all_gather(piece, "pcol", axis=0, tiled=False)
    every = every.reshape(ratio, panels, piece.shape[0], width)
    columns = [every[:, k].reshape(column.shape) for k in range(panels)]
    row_blocks = jnp.concatenate(
        [jnp.arange(panels, dtype=jnp.int32), jnp.arange(nrows, dtype=jnp.int32) * prows + p]
    )
    col_blocks = jnp.arange(ncols, dtype=jnp.int32) * pcols + q
    corner = panels * width
    lowers, uppers = [], []
    mine = work[:, :width]
    for k in range(panels):
        here = columns[k]
        for m in range(k):
            keep = (upper_fill[m, k] == 1).astype(jnp.float32)
            part = here[m * width : (m + 1) * width] * keep
            here = here - mm(lowers[m], part)
        columns[k] = here
        row_keep = jnp.repeat(keep_of(lower_fill[k], k, row_blocks), width)[:, None]
        lower = jnp.where(row_keep, mm(here, inverses[k]), 0.0)
        lowers.append(lower)
        row = tops[k * width : (k + 1) * width]
        for m in range(k):
            row = row - mm(lower_rows(lowers[m], k, width), uppers[m])
        col_keep = jnp.repeat(keep_of(upper_fill[k], k, col_blocks), width)[None, :]
        uppers.append(jnp.where(col_keep, row, 0.0))
    left = jnp.concatenate([x[corner:] for x in lowers], axis=1)
    out = work - mm(left, jnp.concatenate(uppers, axis=0))
    row_ids = jnp.repeat(row_blocks[panels:], width)[:, None]
    first = out[:, :width]
    for k in range(panels):
        first = jnp.where((q == k) & (row_ids > k), lowers[k][corner:], first)
    out = out.at[:, :width].set(first)
    return out.reshape(nrows, 1, width, ncols, 1, width)


def lower_rows(lower, k, width):
    return lower[k * width : (k + 1) * width]


MESH = pl.DeviceIdType.MESH


def exchange_kernel(
    nrows, width, sending, taking, mat, work, tops, cols,
    send, recv0, recv1, recv2, a2a_send, a2a_recv, ag_send, ag_recv, x_send, x_recv, y_send, y_recv,
    s_send, s_recv, local_sem,
):
    p = lax.axis_index("prow")
    q = lax.axis_index("pcol")
    side, across, core = q // 4, q // 2 % 2, q % 2
    xq = side * 4 + (1 - across) * 2 + core
    yq = (1 - side) * 4 + across * 2 + core
    sq = side * 4 + across * 2 + (1 - core)
    local_rows = nrows * width
    share = local_rows // 4
    top = 2 * width
    size = 4 * width
    others = [((p + t) % 4, q) for t in (2, 1, 3)]

    recv = (recv0, recv1, recv2)
    barrier = pltpu.get_barrier_semaphore()
    for peer in others + [(p, xq), (p, yq), (p, sq)]:
        pl.semaphore_signal(barrier, inc=1, device_id=peer, device_id_type=MESH)
    pl.semaphore_wait(barrier, 6)

    def remote(src, dst, send_sem, recv_sem, peer):
        return pltpu.make_async_remote_copy(
            src_ref=src, dst_ref=dst, send_sem=send_sem, recv_sem=recv_sem,
            device_id=peer, device_id_type=MESH,
        )

    def pick(dst, index, index_base, source, pitch, offset, count):
        unroll = 8

        def group(g, carry):
            for u in range(unroll):
                row = index[index_base + g * unroll + u]
                dst[pl.ds(g * (2 * unroll) + 2 * u, 2), :] = source[
                    pl.ds(row * pitch + offset, 2), :
                ]
            return carry

        lax.fori_loop(0, count // unroll, group, 0)

    def a2a(c, slot):
        peer = others[slot]
        here = recv[c].at[pl.ds(pl.multiple_of(p * (2 * share), 8), 2 * share)]
        return remote(send.at[c, slot], here, a2a_send.at[c, slot], a2a_recv.at[c, slot], peer)

    def scatter_chunk(c):
        for slot in range(3):
            base = others[slot][0] * share
            pick(send.at[c, slot], sending, base, mat, 6, 2 * c, share)
            a2a(c, slot).start()
        mine = recv[c].at[pl.ds(pl.multiple_of(p * (2 * share), 8), 2 * share)]
        pick(mine, sending, p * share, mat, 6, 2 * c, share)

    def collect_chunk(c):
        for slot in range(3):
            a2a(c, slot).wait_recv()
        pick(work.at[c], taking, 0, recv[c], 2, 0, local_rows)

    def top_of(c, owner):
        return tops.at[c, pl.ds(pl.multiple_of(owner * top, 8), top)]

    def gather_own(c):
        own = work.at[c, pl.ds(0, top)]
        copy = pltpu.make_async_copy(own, top_of(c, p), local_sem.at[c])
        copy.start()

        @pl.when(p < 3)
        def _():
            remote(own, top_of(c, p), ag_send.at[c, 0, 0], ag_recv.at[c, 0, 0], (p + 1, q)).start()

        @pl.when(p > 0)
        def _():
            remote(own, top_of(c, p), ag_send.at[c, 1, 0], ag_recv.at[c, 1, 0], (p - 1, q)).start()

    def gather_pass(c, dist):
        for way, step in ((0, 1), (1, -1)):
            owner = p - step * dist
            ahead = p + step

            @pl.when((owner >= 0) & (owner <= 3))
            def _():
                here = top_of(c, owner)
                remote(
                    here, here, ag_send.at[c, way, dist], ag_recv.at[c, way, dist - 1], (p, xq)
                ).wait_recv()

                @pl.when((ahead >= 0) & (ahead <= 3))
                def _():
                    remote(
                        here, here, ag_send.at[c, way, dist],
                        ag_recv.at[c, way, dist], (ahead, q),
                    ).start()

    def gather_sent(c):
        for way, step in ((0, 1), (1, -1)):
            ahead = p + step
            for dist in range(3):
                owner = p - step * dist

                @pl.when((owner >= 0) & (owner <= 3) & (ahead >= 0) & (ahead <= 3))
                def _():
                    here = top_of(c, owner)
                    remote(
                        here, here, ag_send.at[c, way, dist], ag_recv.at[c, way, dist], (p, xq)
                    ).wait_send()

        pltpu.make_async_copy(work.at[c, pl.ds(0, top)], top_of(c, p), local_sem.at[c]).wait()

    straight = across * 2 + core
    cross = (1 - across) * 2 + core
    spots = [4 * top + 0, 4 * top + size, 4 * top + 2 * size, 0, size]

    def place(block, piece):
        return cols.at[block, pl.ds(spots[piece], size)]

    def first_source(piece):
        if piece < 3:
            return work.at[0, pl.ds(piece * size, size)]
        return tops.at[0, pl.ds((piece - 3) * size, size)]

    def to_x(src, piece):
        return remote(src, place(straight, piece), x_send.at[piece], x_recv.at[piece], (p, xq))

    def to_y(src, piece):
        return remote(src, place(straight, piece), y_send.at[piece], y_recv.at[piece], (p, yq))

    def to_s(src, kind, piece):
        block = (straight, cross)[kind]
        return remote(
            src, place(block, piece), s_send.at[kind, piece], s_recv.at[kind, piece], (p, sq)
        )

    def keep_own(piece):
        return pltpu.make_async_copy(
            first_source(piece), place(straight, piece), local_sem.at[3 + piece]
        )

    def column_start(piece):
        @pl.when(side == 0)
        def _():
            src = first_source(piece)
            to_y(src, piece).start()
            to_x(src, piece).start()
            to_s(src, 0, piece).start()
            keep_own(piece).start()

    def column_pass(piece):
        @pl.when(side == 1)
        def _():
            here = place(straight, piece)
            to_y(here, piece).wait_recv()
            to_x(here, piece).start()
            to_s(here, 0, piece).start()

        here = place(cross, piece)
        remote(here, here, x_send.at[piece], x_recv.at[piece], (p, xq)).wait_recv()
        to_s(here, 1, piece).start()

    def column_end(piece):
        for kind in range(2):
            block = (straight, cross)[kind]
            theirs = place(block + 1 - 2 * core, piece)
            remote(
                theirs, theirs, s_send.at[kind, piece], s_recv.at[kind, piece], (p, sq)
            ).wait_recv()
            to_s(theirs, kind, piece).wait_send()
        to_x(place(straight, piece), piece).wait_send()

        @pl.when(side == 0)
        def _():
            to_y(place(straight, piece), piece).wait_send()
            keep_own(piece).wait()

    scatter_chunk(0)
    scatter_chunk(1)
    collect_chunk(0)
    for piece in range(3):
        column_start(piece)
    gather_own(0)
    scatter_chunk(2)
    column_pass(0)
    column_pass(1)
    collect_chunk(1)
    gather_own(1)
    gather_pass(0, 1)
    column_pass(2)
    gather_pass(0, 2)
    gather_pass(0, 3)
    gather_sent(0)
    column_start(3)
    column_start(4)
    collect_chunk(2)
    gather_own(2)
    for dist in (1, 2, 3):
        gather_pass(1, dist)
        gather_pass(2, dist)
    column_pass(3)
    column_pass(4)
    gather_sent(1)
    gather_sent(2)
    for piece in range(5):
        column_end(piece)
    for c in range(3):
        for slot in range(3):
            a2a(c, slot).wait_send()


def exchange(matrix, sending, taking, nrows, width):
    local_rows = nrows * width
    share = local_rows // 4
    dma = pltpu.SemaphoreType.DMA
    vmem = pl.BlockSpec(memory_space=pltpu.VMEM)
    smem = pl.BlockSpec(memory_space=pltpu.SMEM)
    hbm = pl.BlockSpec(memory_space=pl.ANY)
    f32 = jnp.float32
    return pl.pallas_call(
        functools.partial(exchange_kernel, nrows, width),
        out_shape=(
            jax.ShapeDtypeStruct((3, 2 * local_rows, 128), f32),
            jax.ShapeDtypeStruct((3, 8 * width, 128), f32),
            jax.ShapeDtypeStruct((4, 8 * width + 2 * local_rows, 128), f32),
        ),
        in_specs=[smem, smem, vmem],
        out_specs=(vmem, hbm, hbm),
        scratch_shapes=[
            pltpu.VMEM((3, 3, 2 * share, 128), f32),
            pltpu.VMEM((2 * local_rows, 128), f32),
            pltpu.VMEM((2 * local_rows, 128), f32),
            pltpu.VMEM((2 * local_rows, 128), f32),
            dma((3, 3)), dma((3, 3)), dma((3, 2, 4)), dma((3, 2, 4)),
            dma((5,)), dma((5,)), dma((5,)), dma((5,)), dma((2, 5)), dma((2, 5)), dma((8,)),
        ],
        compiler_params=pltpu.CompilerParams(
            collective_id=0, has_side_effects=True, vmem_limit_bytes=60 * 1024 * 1024
        ),
        name="exchange",
    )(sending, taking, matrix)


def halves(x):
    high = x.astype(jnp.bfloat16)
    return high, (x - high.astype(jnp.float32)).astype(jnp.bfloat16)


def dot3(a, b):
    dot = functools.partial(jnp.dot, preferred_element_type=jnp.float32)
    return dot(a[0], b[0]) + (dot(a[0], b[1]) + dot(a[1], b[0]))


def factor_kernel(
    nrows, width, row_keep, col_keep, place_here, work, tops, cols, inv, out, lh, ll, uh, ul, ch, cl
):
    def pairs(ref, lead, start, rows):
        left = ref[lead, pl.ds(start, rows, stride=2), :]
        right = ref[lead, pl.ds(start + 1, rows, stride=2), :]
        return jnp.concatenate([left, right], axis=1)

    def lower_part(start, depth):
        rows = pl.ds(start, width)
        return lh[rows, :depth], ll[rows, :depth]

    corner = 4 * width
    for k in range(4):
        depth = k * width
        inverse = halves(inv[k])

        def finish(h, start, keep):
            low = jnp.where(keep == 1, dot3(halves(h), inverse), 0.0)
            high, rest = halves(low)
            lh[pl.ds(start, width), depth : depth + width] = high
            ll[pl.ds(start, width), depth : depth + width] = rest

        for r in range(4):
            h = pairs(cols, k, 2 * r * width, width)
            take = min(r, k) * width
            if take:
                h = h - dot3(lower_part(r * width, take), (ch[:take, :], cl[:take, :]))
            if r < k:
                high, rest = halves(jnp.where(col_keep[r, 3 + k] == 1, h, 0.0))
                ch[r * width : (r + 1) * width, :] = high
                cl[r * width : (r + 1) * width, :] = rest
            finish(h, r * width, row_keep[k, r])

        def tile(i, carry):
            start = pl.multiple_of(corner + i * width, width)
            h = pairs(cols, k, 2 * start, width)
            if depth:
                h = h - dot3(lower_part(start, depth), (ch[:depth, :], cl[:depth, :]))
            finish(h, start, row_keep[k, 4 + i])
            return carry

        lax.fori_loop(0, nrows, tile, 0)
        for c in range(3):
            span = slice(c * width, (c + 1) * width)
            u = pairs(tops, c, 2 * depth, width)
            if depth:
                u = u - dot3(lower_part(k * width, depth), (uh[:depth, span], ul[:depth, span]))
            high, rest = halves(jnp.where(col_keep[k, c] == 1, u, 0.0))
            uh[depth : depth + width, span] = high
            ul[depth : depth + width, span] = rest

    def update(i, carry):
        start = pl.multiple_of(corner + i * width, width)
        left = lower_part(start, 4 * width)
        for c in range(3):
            span = slice(c * width, (c + 1) * width)
            value = pairs(work, c, 2 * width * i, width) - dot3(left, (uh[:, span], ul[:, span]))
            if c == 0:
                for k in range(4):
                    part = slice(k * width, (k + 1) * width)
                    low = left[0][:, part].astype(jnp.float32) + left[1][:, part].astype(
                        jnp.float32
                    )
                    value = jnp.where(place_here[k, i] == 1, low, value)
            for half in range(2):
                out[pl.ds(i * (6 * width) + 2 * c + half, width, stride=6), :] = value[
                    :, half * 128 : (half + 1) * 128
                ]
        return carry

    lax.fori_loop(0, nrows, update, 0)


def factor(row_keep, col_keep, place_here, work, tops, cols, inverses, nrows, width):
    vmem = pl.BlockSpec(memory_space=pltpu.VMEM)
    smem = pl.BlockSpec(memory_space=pltpu.SMEM)
    rows = (4 + nrows) * width
    bf16 = jnp.bfloat16
    return pl.pallas_call(
        functools.partial(factor_kernel, nrows, width),
        out_shape=jax.ShapeDtypeStruct((nrows * width * 6, 128), jnp.float32),
        in_specs=[smem] * 3 + [vmem] * 4,
        out_specs=vmem,
        scratch_shapes=[
            pltpu.VMEM((rows, 4 * width), bf16), pltpu.VMEM((rows, 4 * width), bf16),
            pltpu.VMEM((4 * width, 3 * width), bf16), pltpu.VMEM((4 * width, 3 * width), bf16),
            pltpu.VMEM((4 * width, width), bf16), pltpu.VMEM((4 * width, width), bf16),
        ],
        compiler_params=pltpu.CompilerParams(vmem_limit_bytes=60 * 1024 * 1024),
        name="factor",
    )(row_keep, col_keep, place_here, work, tops, cols, inverses)


def kernel_body(matrix, row_order, inverses, lower_fill, upper_fill):
    nrows, width = matrix.shape[0], matrix.shape[2]
    p = lax.axis_index("prow")
    q = lax.axis_index("pcol")
    sending, taking = index_lists(row_order, nrows, width, 4, p)
    linear = matrix.reshape(nrows * width * 6, 128)
    work, tops, cols = exchange(linear, sending, taking, nrows, width)
    four = jnp.arange(4, dtype=jnp.int32)
    mine = jnp.arange(nrows, dtype=jnp.int32) * 4 + p
    blocks = jnp.concatenate([four, mine])
    row_keep = ((blocks[None] > four[:, None]) & (lower_fill[:, blocks] == 1)).astype(jnp.int32)
    blocks = jnp.concatenate([jnp.arange(3, dtype=jnp.int32) * 8 + q, four])
    col_keep = ((blocks[None] > four[:, None]) & (upper_fill[:, blocks] == 1)).astype(jnp.int32)
    place_here = ((q == four)[:, None] & (mine[None] > four[:, None])).astype(jnp.int32)
    out = factor(row_keep, col_keep, place_here, work, tops, cols, inverses, nrows, width)
    return out.reshape(matrix.shape)


def solution(mesh):
    in_specs = (P(None, "prow", None, None, "pcol", None), P(), P(), P(), P())
    out_specs = P(None, "prow", None, None, "pcol", None)
    fits = mesh.shape["prow"] == 4 and mesh.shape["pcol"] == 8
    return jax.shard_map(
        kernel_body if fits else body,
        mesh=mesh, in_specs=in_specs, out_specs=out_specs, check_vma=False,
    )
```

profile of v0, /device:TPU:5, one launch (start us, length us, event | category | flops | bytes accessed | tf_op | source)
XLA Modules:
  0.0 251.5 jit_solution(12201639622423217884)
XLA Ops:
  0.1 0.1 fusion.26
  0.1 0.1 pad_add_fusion.1
  0.2 0.1 fusion.25
  0.3 0.1 pad_add_fusion
  0.4 0.6 fusion.24.place_here
  1.0 0.8 copy.11
  1.8 0.6 gather_fusion
  2.4 0.1 copy.18
  2.5 0.6 fusion.20.row_keep
  3.1 0.8 copy.13
  3.8 0.6 gather_fusion.1
  4.4 0.1 copy.19
  4.5 0.6 fusion.22.col_keep
  5.1 0.8 reshape.156
  5.9 5.0 %sort.30 = (s32[1536]{0:T(1024)S(1)}, s32[1536]{0:T(1024)}) sort(s32[1536]{0:T(1024)S(1)} %fusion.17, s32[1536]{0:T(1024)S(1)} %iota.81), dimensions={0}, to_apply=%region_0.1 | sort | flops 16896 | bytes 24576 | tf_op jit(solution)/shard_map/jit(sort)/sort | solution.py:20
  11.0 0.3 reduce-window.9
  11.3 0.1 slice.17
  11.4 0.1 reduce-window.12
  11.5 0.1 slice_reduce_fusion
  11.6 0.1 fusion.5
  11.7 6.8 %sort.31 = (s32[6144]{0:T(1024)S(1)}, s32[6144]{0:T(1024)}) sort(s32[6144]{0:T(1024)S(1)} %fusion.5, s32[6144]{0:T(1024)S(1)} %iota.82), dimensions={0}, to_apply=%region_3.4 | sort | flops 79872 | bytes 98304 | tf_op jit(solution)/shard_map/jit(sort)/sort | solution.py:26
  18.5 0.6 add_select_fusion.6
  19.1 192.5 %exchange.1 = (f32[3,3072,128]{2,1,0:T(8,128)}, f32[3,2048,128]{2,1,0:T(8,128)}, f32[4,5120,128]{2,1,0:T(8,128)}) custom-call(s32[1536]{0:T(1024)} %get-tuple-element.18.sending, s32[1536]{0:T(1024)} %get-tuple-element.17.taking, f32[9216,128]{1,0:T(8,128)} %bitcast.17), custom_call_target="tpu_custom_call" | custom-call | tf_op jit(solution)/shard_map/exchange/pallas_call | solution.py:318
  211.6 39.9 %factor.1 = f32[9216,128]{1,0:T(8,128)} custom-call(s32[4,10]{1,0:T(4,128)} %fusion.20.row_keep, s32[4,7]{1,0:T(4,128)} %fusion.22.col_keep, s32[4,6]{1,0:T(4,128)} %fusion.24.place_here, f32[3,3072,128]{2,1,0:T(8,128)} %get-tuple-element.14.work, f32[3,2048,128]{2,1,0:T(8,128)} %get-tuple-element.15.tops, f32[4,5120,128]{2,1,0:T(8,128)} %get-tuple-element.16.cols, ...), custom_call_target="tpu_custom_call" | custom-call | tf_op jit(solution)/shard_map/factor/pallas_call | solution.py:431
  (22 shorter events, 0.2 us)
where the time goes:
time: 252 us
  Pallas kernels  232 us (92%)
  other arithmetic  15.1 us (6%)
  local copies, waits for them, and re-layouts  3.85 us (2%)
    pallas_call x1, Pallas kernels, exchange(): pl.pallas_call(functools.partial(exchange_kernel, nrows, width), out_shap...  192 us
    pallas_call x1, Pallas kernels, factor(): pl.pallas_call(functools.partial(factor_kernel, nrows, width), out_shape=...  39.9 us
    sort x1, other arithmetic, index_lists(): taking = jnp.sort(key)[:local_rows] % local_rows  6.81 us

commit v1 on v0

--- a/solution.py
+++ b/solution.py
@@ -17,14 +17,15 @@
     blocks = row_order.reshape(rows, prows, width)
     targets = lax.dynamic_index_in_dim(blocks, here_row, 1, keepdims=False).reshape(-1)
     local = jnp.arange(local_rows, dtype=jnp.int32)
-    sending = jnp.sort((targets // width % prows) * local_rows + local) % local_rows
+    sending = (targets // width % prows) * local_rows + local
     by_source = jnp.transpose(blocks, (1, 0, 2)).reshape(-1)
     dest_local = by_source // width // prows * width + by_source % width
     mine = by_source // width % prows == here_row
     position = jnp.cumsum(mine.astype(jnp.int32)) - 1
     key = jnp.where(mine, dest_local * local_rows + position, local_rows * local_rows)
-    taking = jnp.sort(key)[:local_rows] % local_rows
-    return sending, taking
+    both = jnp.concatenate([sending, prows * local_rows + key])
+    both = lax.sort(both, is_stable=False)[: 2 * local_rows] % local_rows
+    return both[:local_rows], both[local_rows:]
 
 
 def keep_of(fill_row, panel, blocks):
@@ -145,13 +146,14 @@
         here = recv[c].at[pl.ds(pl.multiple_of(p * (2 * share), 8), 2 * share)]
         return remote(send.at[c, slot], here, a2a_send.at[c, slot], a2a_recv.at[c, slot], peer)
 
-    def scatter_chunk(c):
-        for slot in range(3):
+    def scatter_part(c, slots):
+        for slot in slots:
             base = others[slot][0] * share
             pick(send.at[c, slot], sending, base, mat, 6, 2 * c, share)
             a2a(c, slot).start()
-        mine = recv[c].at[pl.ds(pl.multiple_of(p * (2 * share), 8), 2 * share)]
-        pick(mine, sending, p * share, mat, 6, 2 * c, share)
+        if 2 in slots:
+            mine = recv[c].at[pl.ds(pl.multiple_of(p * (2 * share), 8), 2 * share)]
+            pick(mine, sending, p * share, mat, 6, 2 * c, share)
 
     def collect_chunk(c):
         for slot in range(3):
@@ -206,6 +208,7 @@
                         here, here, ag_send.at[c, way, dist], ag_recv.at[c, way, dist], (p, xq)
                     ).wait_send()
 
+    def gather_kept(c):
         pltpu.make_async_copy(work.at[c, pl.ds(0, top)], top_of(c, p), local_sem.at[c]).wait()
 
     straight = across * 2 + core
@@ -273,33 +276,40 @@
             to_y(place(straight, piece), piece).wait_send()
             keep_own(piece).wait()
 
-    scatter_chunk(0)
-    scatter_chunk(1)
+    scatter_part(0, (0, 1, 2))
+    scatter_part(1, (0,))
     collect_chunk(0)
     for piece in range(3):
         column_start(piece)
     gather_own(0)
-    scatter_chunk(2)
+    scatter_part(1, (1, 2))
     column_pass(0)
+    gather_pass(0, 1)
+    scatter_part(2, (0,))
     column_pass(1)
+    gather_pass(0, 2)
+    scatter_part(2, (1, 2))
     collect_chunk(1)
     gather_own(1)
-    gather_pass(0, 1)
     column_pass(2)
-    gather_pass(0, 2)
     gather_pass(0, 3)
-    gather_sent(0)
+    gather_kept(0)
     column_start(3)
     column_start(4)
+    gather_pass(1, 1)
     collect_chunk(2)
     gather_own(2)
-    for dist in (1, 2, 3):
-        gather_pass(1, dist)
-        gather_pass(2, dist)
+    gather_pass(1, 2)
     column_pass(3)
+    gather_pass(2, 1)
+    gather_pass(1, 3)
+    gather_pass(2, 2)
     column_pass(4)
-    gather_sent(1)
-    gather_sent(2)
+    gather_pass(2, 3)
+    gather_kept(1)
+    gather_kept(2)
+    for c in range(3):
+        gather_sent(c)
     for piece in range(5):
         column_end(piece)
     for c in range(3):
@@ -344,76 +354,85 @@
     return high, (x - high.astype(jnp.float32)).astype(jnp.bfloat16)
 
 
-def dot3(a, b):
-    dot = functools.partial(jnp.dot, preferred_element_type=jnp.float32)
-    return dot(a[0], b[0]) + (dot(a[0], b[1]) + dot(a[1], b[0]))
+def left3(x):
+    high, rest = halves(x)
+    return jnp.concatenate([high, high, rest], axis=1)
+
+
+def right3(x):
+    high, rest = halves(x)
+    return jnp.concatenate([high, rest, high], axis=0)
 
 
 def factor_kernel(
-    nrows, width, row_keep, col_keep, place_here, work, tops, cols, inv, out, lh, ll, uh, ul, ch, cl
+    nrows, width, lower_fill, upper_fill, work, tops, cols, inv, out, l3, u3, c3
 ):
+    p = lax.axis_index("prow")
+    q = lax.axis_index("pcol")
+
+    def dot(a, b):
+        return jnp.dot(a, b, preferred_element_type=jnp.float32)
+
+    def kept(fill, k, block):
+        return (block > k) & (fill[k, block] == 1)
+
     def pairs(ref, lead, start, rows):
         left = ref[lead, pl.ds(start, rows, stride=2), :]
         right = ref[lead, pl.ds(start + 1, rows, stride=2), :]
         return jnp.concatenate([left, right], axis=1)
 
-    def lower_part(start, depth):
-        rows = pl.ds(start, width)
-        return lh[rows, :depth], ll[rows, :depth]
-
     corner = 4 * width
     for k in range(4):
-        depth = k * width
-        inverse = halves(inv[k])
+        deep = 3 * k * width
+        inverse = right3(inv[k])
 
         def finish(h, start, keep):
-            low = jnp.where(keep == 1, dot3(halves(h), inverse), 0.0)
-            high, rest = halves(low)
-            lh[pl.ds(start, width), depth : depth + width] = high
-            ll[pl.ds(start, width), depth : depth + width] = rest
+            low = jnp.where(keep, dot(left3(h), inverse), 0.0)
+            l3[pl.ds(start, width), deep : deep + 3 * width] = left3(low)
 
         for r in range(4):
             h = pairs(cols, k, 2 * r * width, width)
-            take = min(r, k) * width
+            take = 3 * min(r, k) * width
             if take:
-                h = h - dot3(lower_part(r * width, take), (ch[:take, :], cl[:take, :]))
+                h = h - dot(l3[r * width : (r + 1) * width, :take], c3[:take, :])
             if r < k:
-                high, rest = halves(jnp.where(col_keep[r, 3 + k] == 1, h, 0.0))
-                ch[r * width : (r + 1) * width, :] = high
-                cl[r * width : (r + 1) * width, :] = rest
-            finish(h, r * width, row_keep[k, r])
+                c3[3 * r * width : 3 * (r + 1) * width, :] = right3(
+                    jnp.where(kept(upper_fill, r, k), h, 0.0)
+                )
+            finish(h, r * width, kept(lower_fill, k, r))
 
         def tile(i, carry):
             start = pl.multiple_of(corner + i * width, width)
             h = pairs(cols, k, 2 * start, width)
-            if depth:
-                h = h - dot3(lower_part(start, depth), (ch[:depth, :], cl[:depth, :]))
-            finish(h, start, row_keep[k, 4 + i])
+            if deep:
+                h = h - dot(l3[pl.ds(start, width), :deep], c3[:deep, :])
+            finish(h, start, kept(lower_fill, k, i * 4 + p))
             return carry
 
         lax.fori_loop(0, nrows, tile, 0)
         for c in range(3):
             span = slice(c * width, (c + 1) * width)
-            u = pairs(tops, c, 2 * depth, width)
-            if depth:
-                u = u - dot3(lower_part(k * width, depth), (uh[:depth, span], ul[:depth, span]))
-            high, rest = halves(jnp.where(col_keep[k, c] == 1, u, 0.0))
-            uh[depth : depth + width, span] = high
-            ul[depth : depth + width, span] = rest
+            u = pairs(tops, c, 2 * k * width, width)
+            if deep:
+                u = u - dot(l3[k * width : (k + 1) * width, :deep], u3[:deep, span])
+            u3[deep : deep + 3 * width, span] = right3(
+                jnp.where(kept(upper_fill, k, c * 8 + q), u, 0.0)
+            )
 
     def update(i, carry):
         start = pl.multiple_of(corner + i * width, width)
-        left = lower_part(start, 4 * width)
         for c in range(3):
             span = slice(c * width, (c + 1) * width)
-            value = pairs(work, c, 2 * width * i, width) - dot3(left, (uh[:, span], ul[:, span]))
+            value = pairs(work, c, 2 * width * i, width) - dot(
+                l3[pl.ds(start, width), :], u3[:, span]
+            )
             if c == 0:
                 for k in range(4):
-                    part = slice(k * width, (k + 1) * width)
-                    low = left[0][:, part].astype(jnp.float32) + left[1][:, part].astype(
-                        jnp.float32
-                    )
-                    value = jnp.where(place_here[k, i] == 1, low, value)
+                    deep = 3 * k * width
+                    high = l3[pl.ds(start, width), deep : deep + width].astype(jnp.float32)
+                    rest = l3[pl.ds(start, width), deep + 2 * width : deep + 3 * width]
+                    low = high + rest.astype(jnp.float32)
+                    value = jnp.where((q == k) & (i * 4 + p > k), low, value)
             for half in range(2):
                 out[pl.ds(i * (6 * width) + 2 * c + half, width, stride=6), :] = value[
                     :, half * 128 : (half + 1) * 128
@@ -423,7 +442,7 @@
     lax.fori_loop(0, nrows, update, 0)
 
 
-def factor(row_keep, col_keep, place_here, work, tops, cols, inverses, nrows, width):
+def factor(lower_fill, upper_fill, work, tops, cols, inverses, nrows, width):
     vmem = pl.BlockSpec(memory_space=pltpu.VMEM)
     smem = pl.BlockSpec(memory_space=pltpu.SMEM)
     rows = (4 + nrows) * width
@@ -431,33 +450,25 @@
     return pl.pallas_call(
         functools.partial(factor_kernel, nrows, width),
         out_shape=jax.ShapeDtypeStruct((nrows * width * 6, 128), jnp.float32),
-        in_specs=[smem] * 3 + [vmem] * 4,
+        in_specs=[smem] * 2 + [vmem] * 4,
         out_specs=vmem,
         scratch_shapes=[
-            pltpu.VMEM((rows, 4 * width), bf16), pltpu.VMEM((rows, 4 * width), bf16),
-            pltpu.VMEM((4 * width, 3 * width), bf16), pltpu.VMEM((4 * width, 3 * width), bf16),
-            pltpu.VMEM((4 * width, width), bf16), pltpu.VMEM((4 * width, width), bf16),
+            pltpu.VMEM((rows, 12 * width), bf16),
+            pltpu.VMEM((12 * width, 3 * width), bf16),
+            pltpu.VMEM((12 * width, width), bf16),
         ],
         compiler_params=pltpu.CompilerParams(vmem_limit_bytes=60 * 1024 * 1024),
         name="factor",
-    )(row_keep, col_keep, place_here, work, tops, cols, inverses)
+    )(lower_fill, upper_fill, work, tops, cols, inverses)
 
 
 def kernel_body(matrix, row_order, inverses, lower_fill, upper_fill):
     nrows, width = matrix.shape[0], matrix.shape[2]
     p = lax.axis_index("prow")
-    q = lax.axis_index("pcol")
     sending, taking = index_lists(row_order, nrows, width, 4, p)
     linear = matrix.reshape(nrows * width * 6, 128)
     work, tops, cols = exchange(linear, sending, taking, nrows, width)
-    four = jnp.arange(4, dtype=jnp.int32)
-    mine = jnp.arange(nrows, dtype=jnp.int32) * 4 + p
-    blocks = jnp.concatenate([four, mine])
-    row_keep = ((blocks[None] > four[:, None]) & (lower_fill[:, blocks] == 1)).astype(jnp.int32)
-    blocks = jnp.concatenate([jnp.arange(3, dtype=jnp.int32) * 8 + q, four])
-    col_keep = ((blocks[None] > four[:, None]) & (upper_fill[:, blocks] == 1)).astype(jnp.int32)
-    place_here = ((q == four)[:, None] & (mine[None] > four[:, None])).astype(jnp.int32)
-    out = factor(row_keep, col_keep, place_here, work, tops, cols, inverses, nrows, width)
+    out = factor(lower_fill, upper_fill, work, tops, cols, inverses, nrows, width)
     return out.reshape(matrix.shape)
 
 

time: 252 us -> 218 us (0.87)
  Pallas kernels: 232 us -> 210 us
  other arithmetic: 15.1 us -> 6.13 us
    pallas_call x1, Pallas kernels: 192 us -> 174 us  [exchange(): pl.pallas_call(functools.partial(exchange_kernel, nrows, width), out_shap...]
    sort x2 -> x1, other arithmetic: 11.8 us -> 5.6 us  [index_lists(): both = lax.sort(both, is_stable=False)[:2 * local_rows] % local_rows]
    pallas_call x1, Pallas kernels: 39.9 us -> 37 us  [factor(): pl.pallas_call(functools.partial(factor_kernel, nrows, width), out_shape=...]
where the time goes in v1:
time: 218 us
  Pallas kernels  210 us (96%)
  other arithmetic  6.13 us (3%)
    pallas_call x1, Pallas kernels, exchange(): pl.pallas_call(functools.partial(exchange_kernel, nrows, width), out_shap...  174 us
    pallas_call x1, Pallas kernels, factor(): pl.pallas_call(functools.partial(factor_kernel, nrows, width), out_shape=...  37 us
    sort x1, other arithmetic, index_lists(): both = lax.sort(both, is_stable=False)[:2 * local_rows] % local_rows  5.6 us

profile of v1, /device:TPU:5, one launch (start us, length us, event | category | flops | bytes accessed | tf_op | source)
XLA Modules:
  0.0 218.3 jit_solution(2713662322308770408)
XLA Ops:
  0.0 0.8 reshape.45
  0.9 0.3 reduce-window.9
  1.2 0.1 slice.21
  1.3 0.1 reduce-window.12
  1.3 0.1 slice_reduce_fusion
  1.5 0.1 fusion.6
  1.6 5.6 %sort.7 = s32[7680]{0:T(1024)S(1)} sort(s32[7680]{0:T(1024)S(1)} %pad_add_fusion), dimensions={0}, to_apply=%region_2.3 | sort | flops 99840 | bytes 61440 | tf_op jit(solution)/shard_map/sort | solution.py:27
  7.2 0.6 fusion.20
  7.8 173.5 %exchange.1 = (f32[3,3072,128]{2,1,0:T(8,128)}, f32[3,2048,128]{2,1,0:T(8,128)}, f32[4,5120,128]{2,1,0:T(8,128)}) custom-call(s32[1536]{0:T(1024)} %get-tuple-element.12.sending, s32[1536]{0:T(1024)} %get-tuple-element.11.taking, f32[9216,128]{1,0:T(8,128)} %bitcast.5), custom_call_target="tpu_custom_call" | custom-call | tf_op jit(solution)/shard_map/exchange/pallas_call | solution.py:328
  181.3 37.0 %factor.1 = f32[9216,128]{1,0:T(8,128)} custom-call(s32[4,24]{1,0:T(4,128)} %lower_fill.1, s32[4,24]{1,0:T(4,128)} %upper_fill.1, f32[3,3072,128]{2,1,0:T(8,128)} %get-tuple-element.8.work, f32[3,2048,128]{2,1,0:T(8,128)} %get-tuple-element.9.tops, f32[4,5120,128]{2,1,0:T(8,128)} %get-tuple-element.10.cols, f32[4,256,256]{2,1,0:T(8,128)} %inv.1), custom_call_target="tpu_custom_call" | custom-call | tf_op jit(solution)/shard_map/factor/pallas_call | solution.py:450
  (9 shorter events, 0.1 us)

commit v2 on v1

--- a/solution.py
+++ b/solution.py
@@ -365,8 +365,20 @@
 
 
 def factor_kernel(
-    nrows, width, lower_fill, upper_fill, work, tops, cols, inv, out, l3, u3, c3
+    nrows, width, lower_fill, upper_fill, work_in, tops_in, cols_in, inv, out, l3, u3, c3,
+    work, tops, cols, sems,
 ):
+    col_copies = [
+        pltpu.make_async_copy(cols_in.at[k], cols.at[k], sems.at[k]) for k in range(4)
+    ]
+    top_copies = [
+        pltpu.make_async_copy(tops_in.at[c], tops.at[c], sems.at[4 + c]) for c in range(3)
+    ]
+    work_copies = [
+        pltpu.make_async_copy(work_in.at[c], work.at[c], sems.at[7 + c]) for c in range(3)
+    ]
+    for copy in col_copies[:1] + top_copies + col_copies[1:] + work_copies:
+        copy.start()
     p = lax.axis_index("prow")
     q = lax.axis_index("pcol")
 
@@ -385,6 +397,7 @@
     for k in range(4):
         deep = 3 * k * width
         inverse = right3(inv[k])
+        col_copies[k].wait()
 
         def finish(h, start, keep):
             low = jnp.where(keep, dot(left3(h), inverse), 0.0)
@@ -412,6 +425,8 @@
         lax.fori_loop(0, nrows, tile, 0)
         for c in range(3):
             span = slice(c * width, (c + 1) * width)
+            if k == 0:
+                top_copies[c].wait()
             u = pairs(tops, c, 2 * k * width, width)
             if deep:
                 u = u - dot(l3[k * width : (k + 1) * width, :deep], u3[:deep, span])
@@ -439,6 +454,8 @@
                 ]
         return carry
 
+    for copy in work_copies:
+        copy.wait()
     lax.fori_loop(0, nrows, update, 0)
 
 
@@ -450,12 +467,16 @@
     return pl.pallas_call(
         functools.partial(factor_kernel, nrows, width),
         out_shape=jax.ShapeDtypeStruct((nrows * width * 6, 128), jnp.float32),
-        in_specs=[smem] * 2 + [vmem] * 4,
+        in_specs=[smem] * 2 + [pl.BlockSpec(memory_space=pl.ANY)] * 3 + [vmem],
         out_specs=vmem,
         scratch_shapes=[
             pltpu.VMEM((rows, 12 * width), bf16),
             pltpu.VMEM((12 * width, 3 * width), bf16),
             pltpu.VMEM((12 * width, width), bf16),
+            pltpu.VMEM(work.shape, jnp.float32),
+            pltpu.VMEM(tops.shape, jnp.float32),
+            pltpu.VMEM(cols.shape, jnp.float32),
+            pltpu.SemaphoreType.DMA((10,)),
         ],
         compiler_params=pltpu.CompilerParams(vmem_limit_bytes=60 * 1024 * 1024),
         name="factor",

time: 218 us -> 216 us (level)
    pallas_call x1, Pallas kernels: 37 us -> 34.4 us  [factor(): pl.pallas_call(functools.partial(factor_kernel, nrows, width), out_shape=...]
where the time goes in v2:
time: 216 us
  Pallas kernels  208 us (96%)
  other arithmetic  6.13 us (3%)
    pallas_call x1, Pallas kernels, exchange(): pl.pallas_call(functools.partial(exchange_kernel, nrows, width), out_shap...  174 us
    pallas_call x1, Pallas kernels, factor(): pl.pallas_call(functools.partial(factor_kernel, nrows, width), out_shape=...  34.4 us
    sort x1, other arithmetic, index_lists(): both = lax.sort(both, is_stable=False)[:2 * local_rows] % local_rows  5.6 us

profile of v2, /device:TPU:5, one launch (start us, length us, event | category | flops | bytes accessed | tf_op | source)
XLA Modules:
  0.0 215.8 jit_solution(1488092597205971817)
XLA Ops:
  0.0 0.8 reshape.45
  0.9 0.3 reduce-window.9
  1.2 0.1 slice.21
  1.3 0.1 reduce-window.12
  1.3 0.1 slice_reduce_fusion
  1.5 0.1 fusion.6
  1.6 5.6 %sort.7 = s32[7680]{0:T(1024)S(1)} sort(s32[7680]{0:T(1024)S(1)} %pad_add_fusion), dimensions={0}, to_apply=%region_2.3 | sort | flops 99840 | bytes 61440 | tf_op jit(solution)/shard_map/sort | solution.py:27
  7.2 0.6 fusion.20
  7.8 173.5 %exchange.1 = (f32[3,3072,128]{2,1,0:T(8,128)}, f32[3,2048,128]{2,1,0:T(8,128)}, f32[4,5120,128]{2,1,0:T(8,128)}) custom-call(s32[1536]{0:T(1024)} %get-tuple-element.12.sending, s32[1536]{0:T(1024)} %get-tuple-element.11.taking, f32[9216,128]{1,0:T(8,128)} %bitcast.5), custom_call_target="tpu_custom_call" | custom-call | tf_op jit(solution)/shard_map/exchange/pallas_call | solution.py:328
  181.3 34.4 %factor.1 = f32[9216,128]{1,0:T(8,128)} custom-call(s32[4,24]{1,0:T(4,128)} %lower_fill.1, s32[4,24]{1,0:T(4,128)} %upper_fill.1, f32[3,3072,128]{2,1,0:T(8,128)} %get-tuple-element.8.work_in, f32[3,2048,128]{2,1,0:T(8,128)} %get-tuple-element.9.tops_in, f32[4,5120,128]{2,1,0:T(8,128)} %get-tuple-element.10.cols_in, f32[4,256,256]{2,1,0:T(8,128)} %inv.1), custom_call_target="tpu_custom_call" | custom-call | tf_op jit(solution)/shard_map/factor/pallas_call | solution.py:467
  (9 shorter events, 0.1 us)
